TPU v7x, 32 devices: a whole 2x2x4 slice. The times are simulated.
32 devices in a mesh: grp: 8 (over z, core), atm: 4 (over y, x).
Axes of the slice: x: 2, y: 2, z: 4, core: 2. Of those that a mesh axis runs over, the one named last changes fastest.
Arguments:
- atoms: float32 [2, 8192, 128], P(None, ('grp', 'atm')), may hold values from -6 to 6
- kinds: int32 [2, 8192], P(None, ('grp', 'atm')), may hold values from 0 to 3
- member: int32 [2, 8192], P(None, ('grp', 'atm')), may hold values from 0 to 7
- targets: float32 [2, 64], replicated, may hold values from -900 to 900
- weights: float32 [128, 128], replicated, may hold values from -0.5 to 0.5
- bias: float32 [128], replicated, may hold values from -0.5 to 0.5
- readout: float32 [4, 128], replicated, may hold values from -0.5 to 0.5
- covariance: float32 [16384, 16384], P('grp', 'atm'), as said below
Outputs:
- posterior: float32 [16384, 16384], P('grp', 'atm')
- weights_out: float32 [128, 128], replicated
Inputs may be any that keep to these rules, and one draw needn't show every extreme that they name: `covariance`: symmetric and positive definite.
All inputs are finite; a program needn't handle non-finite values.
Results may differ from a plain program's by a relative error of at most 0.0007.
Values sent between devices are 32-bit elements; how exact they have to be, the bound alone decides.
A program may use at most 128 MiB of HBM per device.

v0:
```python
import jax
import jax.numpy as jnp
from jax import lax
from jax.sharding import PartitionSpec as P

FEATURES = 128
GROUP_LOCAL = 8
STEPS = 2


forget_rate = 0.98


def local_terms(atoms, kinds, member, weights, bias, readout):
    precise = lax.Precision.HIGHEST
    preact = jnp.dot(atoms, weights, precision=precise, preferred_element_type=jnp.float32) + bias
    hidden = jnp.tanh(preact)
    type_hot = (kinds[:, None] == jnp.arange(readout.shape[0])[None, :]).astype(jnp.float32)
    vectors = jnp.dot(type_hot, readout, precision=precise)
    atom_energy = jnp.sum(hidden * vectors, axis=1)
    slope = (1.0 - hidden * hidden) * vectors
    group_hot = (member[:, None] == jnp.arange(GROUP_LOCAL)[None, :]).astype(jnp.float32)
    energies = jnp.dot(atom_energy, group_hot, precision=precise)
    masked = atoms[:, None, :] * group_hot[:, :, None]
    grads = jnp.einsum("agi,ac->gic", masked, slope, precision=precise)
    return (energies, grads.reshape(GROUP_LOCAL, FEATURES * FEATURES))


def body(atoms, kinds, member, targets, weights, bias, readout, covariance):
    precise = lax.Precision.HIGHEST
    row_index = lax.axis_index("grp")
    col_index = lax.axis_index("atm")
    group_total = GROUP_LOCAL * lax.axis_size("grp")
    col_width = covariance.shape[1]
    identity = jnp.eye(group_total, dtype=jnp.float32)
    current = weights
    covar = covariance
    for update_idx in range(STEPS):
        energies, partial_value = local_terms(
            atoms[update_idx], kinds[update_idx], member[update_idx], current, bias, readout
        )
        spread = jnp.zeros((group_total,), jnp.float32)
        spread = lax.dynamic_update_slice_in_dim(spread, energies, row_index * GROUP_LOCAL, 0)
        predicted = lax.psum(spread, ("grp", "atm"))
        mismatch = targets[update_idx] - predicted
        grad_block = lax.psum_scatter(partial_value, "atm", scatter_dimension=1, tiled=True)
        grad_columns = lax.all_gather(grad_block, "grp", axis=0, tiled=True)
        row_terms = lax.dot_general(
            covar,
            grad_columns,
            (((1,), (1,)), ((), ())),
            precision=precise,
            preferred_element_type=jnp.float32,
        )
        row_gains = lax.psum(row_terms, "atm")
        full_gains = lax.all_gather(row_gains, "grp", axis=0, tiled=True)
        col_gains = lax.dynamic_slice_in_dim(full_gains, col_index * col_width, col_width, 0)
        curvature = lax.psum(jnp.dot(grad_columns, col_gains, precision=precise), "atm")
        innovation = 0.5 * (curvature + curvature.T) + forget_rate * identity
        factor = jnp.linalg.cholesky(innovation)
        inverse = jax.scipy.linalg.cho_solve((factor, True), identity)
        coefficient = jnp.dot(inverse, mismatch, precision=precise)
        change = jnp.dot(full_gains, coefficient, precision=precise)
        current = current + change.reshape(FEATURES, FEATURES)
        scaled = jnp.dot(row_gains, inverse, precision=precise)
        downdate = lax.dot_general(
            scaled,
            col_gains,
            (((1,), (1,)), ((), ())),
            precision=precise,
            preferred_element_type=jnp.float32,
        )
        covar = (covar - downdate) / forget_rate
    return (covar, current)


def solution(mesh):
    return jax.shard_map(
        body,
        mesh=mesh,
        in_specs=(
            P(None, ("grp", "atm"), None),
            P(None, ("grp", "atm")),
            P(None, ("grp", "atm")),
            P(),
            P(),
            P(),
            P(),
            P("grp", "atm"),
        ),
        out_specs=(P("grp", "atm"), P()),
        check_vma=False,
    )
```

profile of v0, /device:TPU:0, one launch (start us, length us, event | category | flops | bytes accessed | tf_op | source)
XLA Modules:
  0.0 508.2 jit_solution(2378778925858952813)
XLA Ops:
  7.3 0.8 fusion.59
  8.8 1.0 slice_bitcast_fusion
  10.2 1.3 multiply_reduce_fusion.1
  11.5 1.0 convolution_bitcast_fusion.2
  12.5 1.1 copy.27
  13.7 27.9 %reduce-scatter.3.cloned.1.call-done = f32[8,4096]{1,0:T(8,128)} async-done(((f32[8,16384]{1,0:T(8,128)}), f32[8,4096]{1,0:T(8,128)}) %reduce-scatter.3.cloned.1.call-update) | async-done | bytes 131088 | tf_op jit(solution)/shard_map/reduce_scatter | solution.py:46
  41.7 23.8 %all-gather.5.cloned.1.call-done = f32[64,4096]{1,0:T(8,128)} async-done(((f32[8,4096]{1,0:T(8,128)}), f32[64,4096]{1,0:T(8,128)}) %all-gather.5.cloned.1.call-update) | async-done | bytes 1048592 | tf_op jit(solution)/shard_map/all_gather | solution.py:47
  65.5 38.8 %convolution_bitcast_fusion = f32[2048,64]{0,1:T(8,128)} fusion(f32[64,4096]{1,0:T(8,128)} %all-gather.5.cloned.1.call-done, f32[2048,4096]{1,0:T(8,128)} %param.18), kind=kOutput, calls=%fused_computation.2 | convolution fusion | flops 6442450944 | bytes 35127296 | tf_op jit(solution)/shard_map/dot_general | solution.py:48
  104.3 45.0 %all-reduce.3.cloned.1.call-done = f32[2048,64]{0,1:T(8,128)} async-done(((f32[2048,64]{0,1:T(8,128)}), f32[2048,64]{0,1:T(8,128)}) %all-reduce.3.cloned.1.call-update) | async-done | bytes 524304 | tf_op jit(solution)/shard_map/psum | solution.py:55
  149.9 41.8 %psum.44 = f32[64]{0:T(128)S(1)} all-reduce(f32[64]{0:T(128)S(1)} %dynamic_update_slice.6), channel_id=1, replica_groups=mesh['grp'=8,'atm'=4] {'grp','atm'}, use_global_device_ids=true, to_apply=%region_6.0 | all-reduce | flops 64 | bytes 512 | tf_op jit(solution)/shard_map/psum | solution.py:44
  192.0 6.8 %all-gather.7.cloned.1.call-done = f32[16384,64]{0,1:T(8,128)} async-done(((f32[2048,64]{0,1:T(8,128)}), f32[16384,64]{0,1:T(8,128)}) %all-gather.7.cloned.1.call-update) | async-done | bytes 4194320 | tf_op jit(solution)/shard_map/all_gather | solution.py:56
  198.8 2.2 fusion.9
  201.0 16.5 %psum.43 = f32[64,64]{1,0:T(8,128)S(1)} all-reduce(f32[64,64]{1,0:T(8,128)S(1)} %fusion.9), channel_id=1, replica_groups=mesh['grp'=8,'atm'=4] {'atm'}, use_global_device_ids=true, to_apply=%region_2.0 | all-reduce | flops 4096 | bytes 32768 | tf_op jit(solution)/shard_map/psum | solution.py:58
  217.7 5.8 %cholesky.44 = f32[64,64]{1,0:T(8,128)S(1)} custom-call(f32[64,64]{1,0:T(8,128)S(1)} %fusion.43), custom_call_target="Cholesky" | custom-call | tf_op jit(solution)/shard_map/jit(cholesky)/cholesky | solution.py:60
  224.9 4.9 custom-call.8
  230.3 4.5 fusion.62
  235.2 1.0 convolution_bitcast_fusion.1
  236.2 1.1 copy.26
  237.4 2.9 fusion.61
  240.3 19.3 %reduce-scatter.5.cloned.1.call-done = f32[8,4096]{1,0:T(8,128)} async-done(((f32[8,16384]{1,0:T(8,128)}), f32[8,4096]{1,0:T(8,128)}) %reduce-scatter.5.cloned.1.call-update) | async-done | bytes 131088 | tf_op jit(solution)/shard_map/reduce_scatter | solution.py:46
  259.9 34.7 %subtract_multiply_fusion.1 = f32[2048,4096]{1,0:T(8,128)} fusion(f32[2048,4096]{1,0:T(8,128)} %param.18, f32[2048,64]{1,0:T(8,128)S(1)} %fusion.61, f32[16384,64]{0,1:T(8,128)} %all-gather.7.cloned.1.call-done, s32[]{:T(128)S(6)} %select_n.11), kind=kOutput, calls=%fused_computation.1 | convolution fusion | flops 6459228160 | bytes 68681728 | tf_op jit(solution)/shard_map/dot_general | solution.py:66
  294.6 37.0 %fusion.63 = f32[2048,64]{0,1:T(8,128)} fusion(f32[2048,4096]{1,0:T(8,128)} %subtract_multiply_fusion.1, f32[64,4096]{1,0:T(8,128)} %all-gather.9.cloned.1.call-done), kind=kOutput, calls=%fused_computation.101 | convolution fusion | flops 6442450944 | bytes 35127296 | tf_op jit(solution)/shard_map/dot_general | solution.py:48
  331.6 45.5 %all-reduce.5.cloned.1.call-done = f32[2048,64]{0,1:T(8,128)} async-done(((f32[2048,64]{0,1:T(8,128)}), f32[2048,64]{0,1:T(8,128)}) %all-reduce.5.cloned.1.call-update) | async-done | bytes 524304 | tf_op jit(solution)/shard_map/psum | solution.py:55
  377.4 42.0 %psum.47 = f32[64]{0:T(128)S(1)} all-reduce(f32[64]{0:T(128)S(1)} %dynamic_update_slice.7), channel_id=1, replica_groups=mesh['grp'=8,'atm'=4] {'grp','atm'}, use_global_device_ids=true, to_apply=%region_11.14 | all-reduce | flops 64 | bytes 512 | tf_op jit(solution)/shard_map/psum | solution.py:44
  419.5 7.2 %all-gather.11.cloned.1.call-done = f32[16384,64]{0,1:T(8,128)} async-done(((f32[2048,64]{0,1:T(8,128)}), f32[16384,64]{0,1:T(8,128)}) %all-gather.11.cloned.1.call-update) | async-done | bytes 4194320 | tf_op jit(solution)/shard_map/all_gather | solution.py:56
  426.7 2.2 fusion.6
  428.9 16.6 %psum.46 = f32[64,64]{1,0:T(8,128)S(1)} all-reduce(f32[64,64]{1,0:T(8,128)S(1)} %fusion.6), channel_id=1, replica_groups=mesh['grp'=8,'atm'=4] {'atm'}, use_global_device_ids=true, to_apply=%region_9.0 | all-reduce | flops 4096 | bytes 32768 | tf_op jit(solution)/shard_map/psum | solution.py:58
  445.6 5.8 %cholesky.55 = f32[64,64]{1,0:T(8,128)S(1)} custom-call(f32[64,64]{1,0:T(8,128)S(1)} %fusion.38), custom_call_target="Cholesky" | custom-call | tf_op jit(solution)/shard_map/jit(cholesky)/cholesky | solution.py:60
  452.8 4.9 custom-call.9
  458.3 4.5 fusion.65
  463.4 2.9 fusion.64
  466.3 34.7 %subtract_multiply_fusion = f32[2048,4096]{1,0:T(8,128)} fusion(f32[2048,4096]{1,0:T(8,128)} %subtract_multiply_fusion.1, f32[2048,64]{1,0:T(8,128)S(1)} %fusion.64, f32[16384,64]{0,1:T(8,128)} %all-gather.11.cloned.1.call-done, s32[]{:T(128)S(6)} %select_n.11), kind=kOutput, calls=%fused_computation | convolution fusion | flops 6459228160 | bytes 68681728 | tf_op jit(solution)/shard_map/dot_general | solution.py:66
  (69 shorter events, 8.0 us)
Async XLA Ops:
  7.2 2.7 copy-start
  7.2 227.7 %copy-start.4 = (f32[2,256,128]{2,1,0:T(8,128)S(1)}, f32[2,256,128]{2,1,0:T(8,128)}, u32[]{:S(2)}) copy-start(f32[2,256,128]{2,1,0:T(8,128)} %param.11) | copy-start | bytes 786436
  7.2 227.6 %copy-start.5 = (f32[128,128]{1,0:T(8,128)S(1)}, f32[128,128]{1,0:T(8,128)}, u32[]{:S(2)}) copy-start(f32[128,128]{1,0:T(8,128)} %param.15) | copy-start | bytes 196612
  7.2 227.7 %copy-start.7 = (f32[128]{0:T(128)S(1)}, f32[128]{0:T(128)}, u32[]{:S(2)}) copy-start(f32[128]{0:T(128)} %param.16) | copy-start | bytes 1540
  7.2 223.0 %copy-start.6 = (f32[2,64]{1,0:T(2,128)S(1)}, f32[2,64]{1,0:T(2,128)}, u32[]{:S(2)}) copy-start(f32[2,64]{1,0:T(2,128)} %param.14) | copy-start | bytes 1540
  7.2 34.4 %reduce-scatter.3.cloned.1.call-start = ((), (), s32[]{:S(2)}) async-start(), calls=%async_computation.2 | async-start | bytes 655360 | tf_op jit(solution)/shard_map/reduce_scatter | solution.py:46
  13.6 51.8 %all-gather.5.cloned.1.call-start = ((), (), s32[]{:S(2)}) async-start(), calls=%async_computation.3 | async-start | bytes 1179648 | tf_op jit(solution)/shard_map/all_gather | solution.py:47
  41.6 107.7 %all-reduce.3.cloned.1.call-start = ((), (), s32[]{:S(2)}) async-start(), calls=%async_computation.4 | async-start | bytes 1048576 | tf_op jit(solution)/shard_map/psum | solution.py:55
  65.5 133.3 %copy-start.2 = (f32[64,4096]{1,0:T(8,128)S(1)}, f32[64,4096]{1,0:T(8,128)}, u32[]{:S(2)}) copy-start(f32[64,4096]{1,0:T(8,128)} %all-gather.5.cloned.1.call-done) | copy-start | bytes 3145732
  104.3 94.5 %all-gather.7.cloned.1.call-start = ((), (), s32[]{:S(2)}) async-start(), calls=%async_computation.5 | async-start | bytes 4718592 | tf_op jit(solution)/shard_map/all_gather | solution.py:56
  149.4 110.2 %reduce-scatter.5.cloned.1.call-start = ((), (), s32[]{:S(2)}) async-start(), calls=%async_computation.6 | async-start | bytes 655360 | tf_op jit(solution)/shard_map/reduce_scatter | solution.py:46
  237.3 57.2 %all-gather.9.cloned.1.call-start = ((), (), s32[]{:S(2)}) async-start(), calls=%async_computation.7 | async-start | bytes 1179648 | tf_op jit(solution)/shard_map/all_gather | solution.py:47
  259.6 117.5 %all-reduce.5.cloned.1.call-start = ((), (), s32[]{:S(2)}) async-start(), calls=%async_computation.8 | async-start | bytes 1048576 | tf_op jit(solution)/shard_map/psum | solution.py:55
  294.6 132.1 %copy-start.3 = (f32[64,4096]{1,0:T(8,128)S(1)}, f32[64,4096]{1,0:T(8,128)}, u32[]{:S(2)}) copy-start(f32[64,4096]{1,0:T(8,128)} %all-gather.9.cloned.1.call-done) | copy-start | bytes 3145732
  331.6 95.1 %all-gather.11.cloned.1.call-start = ((), (), s32[]{:S(2)}) async-start(), calls=%async_computation.9 | async-start | bytes 4718592 | tf_op jit(solution)/shard_map/all_gather | solution.py:56
  463.4 37.5 %copy-start.1 = (f32[4,128]{1,0:T(4,128)S(1)}, f32[4,128]{1,0:T(4,128)}, u32[]{:S(2)}) copy-start(f32[4,128]{1,0:T(4,128)} %param.17) | copy-start | bytes 6148
Sparse Core Ops, SparseCore 0:
  13.7 27.8 reduce-scatter.2
  43.2 22.2 all-gather.4
  104.4 44.9 all-reduce.2
  150.8 47.9 all-gather.6
  237.5 22.0 reduce-scatter.4
  261.1 22.2 all-gather.8
  331.7 45.3 all-reduce.4
  378.7 47.9 all-gather.10
where the time goes:
time: 516 us; the launch traced here: 508 us
  waiting for transfers between devices  176 us (34%)
  matrix products  170 us (33%)
  blocking collectives  117 us (23%)
  other arithmetic  24.9 us (5%)
  between operations  14.9 us (3%)
  local copies, waits for them, and re-layouts  5.62 us (1%)
    psum x2, waiting for transfers between devices, body(): row_gains = lax.psum(row_terms, 'atm')  90.5 us
    psum x2, blocking collectives, body(): predicted = lax.psum(spread, ('grp', 'atm'))  83.9 us
    dot_general x2, matrix products, body(): lax.dot_general(covar, grad_columns, (((1,), (1,)), ((), ())), precision=...  75.8 us
    dot_general x2, matrix products, body(): lax.dot_general(scaled, col_gains, (((1,), (1,)), ((), ())), precision=pr...  69.3 us
    reduce_scatter x2, waiting for transfers between devices, body(): lax.psum_scatter(partial_value, 'atm', scatter_dimension=1, tiled=True)  47.3 us
    psum x2, blocking collectives, body(): lax.psum(jnp.dot(grad_columns, col_gains, precision=precise), 'atm')  33 us
    all_gather x2, waiting for transfers between devices, body(): grad_columns = lax.all_gather(grad_block, 'grp', axis=0, tiled=True)  23.8 us
    all_gather x2, waiting for transfers between devices, body(): full_gains = lax.all_gather(row_gains, 'grp', axis=0, tiled=True)  14 us
  transfers between devices with their start and end apart: 8, of which 7 were waited for; matrix products, arithmetic and copies ran while one was open for 8% of the time, Pallas kernels for 0%

commit v1 on v0

v1 whole, which is shorter than its diff:
```python
import functools
import jax
import jax.numpy as jnp
from jax import lax
from jax.experimental import pallas as pl
from jax.experimental.pallas import tpu as pltpu
from jax.sharding import PartitionSpec as P

GROUP_LOCAL = 8
STEPS = 2
CORES = 2
LANES = 128

forget_rate = 0.98
precise = lax.Precision.HIGHEST
MESH = pl.DeviceIdType.MESH
VM = pl.BlockSpec(memory_space=pltpu.VMEM)


def local_terms(atoms, kinds, member, weights, bias, readout):
    preact = jnp.dot(atoms, weights, precision=precise, preferred_element_type=jnp.float32) + bias
    hidden = jnp.tanh(preact)
    type_hot = (kinds[:, None] == jnp.arange(readout.shape[0])[None, :]).astype(jnp.float32)
    vectors = jnp.dot(type_hot, readout, precision=precise)
    atom_energy = jnp.sum(hidden * vectors, axis=1)
    slope = (1.0 - hidden * hidden) * vectors
    group_hot = (member[:, None] == jnp.arange(GROUP_LOCAL)[None, :]).astype(jnp.float32)
    energies = jnp.dot(atom_energy, group_hot, precision=precise)
    masked = atoms[:, None, :] * group_hot[:, :, None]
    grads = jnp.einsum("agi,ac->gic", masked, slope, precision=precise)
    return energies, grads.reshape(GROUP_LOCAL, -1)


def push(src, dst, sems, recvs, slot, target):
    copy = pltpu.make_async_remote_copy(
        src_ref=src, dst_ref=dst, send_sem=sems.at[slot], recv_sem=recvs.at[slot],
        device_id=target, device_id_type=MESH,
    )
    copy.start()
    return copy


def greet(targets):
    barrier = pltpu.get_barrier_semaphore()
    for target in targets:
        pl.semaphore_signal(barrier, inc=1, device_id=target, device_id_type=MESH)
    pl.semaphore_wait(barrier, len(targets))


def places(n_grp, n_atm):
    row, col = lax.axis_index("grp"), lax.axis_index("atm")
    n_z = n_grp // CORES
    z, core = row // CORES, lax.rem(row, CORES)
    plane = [lax.rem(col + d, n_atm) for d in range(1, n_atm)]
    column = [lax.rem(z + d, n_z) * CORES + core for d in range(1, n_z)]
    partner = z * CORES + (CORES - 1 - core)
    return row, col, z, core, plane, column, partner


def grads_kernel(n_grp, n_atm, x_ref, out_ref, got, a_s, a_r, b_s, b_r, f_s, f_r):
    row, col, z, core, plane, column, partner = places(n_grp, n_atm)
    greet([{"atm": p} for p in plane] + [{"grp": p} for p in column] + [{"grp": partner}])
    first = [push(x_ref.at[p], got.at[i], a_s, a_r, i, {"atm": p}) for i, p in enumerate(plane)]
    total = x_ref[col]
    for i, copy in enumerate(first):
        copy.wait_recv()
        total = total + got[i]
    out_ref[row] = total
    second = [push(out_ref.at[row], out_ref.at[row], b_s, b_r, i, {"grp": p}) for i, p in enumerate(column)]
    last = [push(out_ref.at[row], out_ref.at[row], f_s, f_r, len(column), {"grp": partner})]
    n_z = n_grp // CORES
    for i, copy in enumerate(second):
        copy.wait_recv()
        origin = lax.rem(z + n_z - (i + 1), n_z) * CORES + core
        last.append(push(out_ref.at[origin], out_ref.at[origin], f_s, f_r, i, {"grp": partner}))
    for copy in last:
        copy.wait_recv()
    for copy in first + second + last:
        copy.wait_send()


def share_grads(x, n_grp, n_atm):
    block = x.shape[1:]
    n_z = n_grp // CORES
    dma = pltpu.SemaphoreType.DMA
    return pl.pallas_call(
        functools.partial(grads_kernel, n_grp, n_atm),
        out_shape=jax.ShapeDtypeStruct((n_grp,) + block, jnp.float32),
        in_specs=[VM], out_specs=VM,
        scratch_shapes=[pltpu.VMEM((n_atm - 1,) + block, jnp.float32)]
        + [dma((n_atm - 1,))] * 2 + [dma((n_z - 1,))] * 2 + [dma((n_z,))] * 2,
        compiler_params=pltpu.CompilerParams(collective_id=0, has_side_effects=True),
        name="share_grads",
    )(x)


def gains_kernel(n_grp, n_atm, half, t_ref, row_ref, col_ref, got, quarter,
                 a_s, a_r, r_s, r_r, b_s, b_r, c_s, c_r, f_s, f_r):
    row, col, z, core, plane, column, partner = places(n_grp, n_atm)
    greet([{"atm": p} for p in plane] + [{"grp": p} for p in column] + [{"grp": partner}])
    first = [push(t_ref.at[p], got.at[i], a_s, a_r, i, {"atm": p}) for i, p in enumerate(plane)]
    total = t_ref[col]
    for i, copy in enumerate(first):
        copy.wait_recv()
        total = total + got[i]
    quarter[z] = total
    row_ref[col] = total
    along = [push(quarter.at[z], quarter.at[z], b_s, b_r, i, {"grp": p}) for i, p in enumerate(column)]
    rows = [push(row_ref.at[col], row_ref.at[col], r_s, r_r, i, {"atm": p}) for i, p in enumerate(plane)]
    for copy in along:
        copy.wait_recv()
    across = [
        push(quarter.at[pl.ds(p * half, half)], col_ref.at[core, col], c_s, c_r, i, {"atm": p})
        for i, p in enumerate(plane)
    ]
    col_ref[core, col] = quarter[pl.ds(col * half, half)]
    last = [push(col_ref.at[core, col], col_ref.at[core, col], f_s, f_r, len(plane), {"grp": partner})]
    for i, copy in enumerate(across):
        copy.wait_recv()
        origin = lax.rem(col + n_atm - (i + 1), n_atm)
        last.append(push(col_ref.at[core, origin], col_ref.at[core, origin], f_s, f_r, i, {"grp": partner}))
    for copy in rows + last:
        copy.wait_recv()
    for copy in first + along + rows + across + last:
        copy.wait_send()


def share_gains(t, n_grp, n_atm):
    _, groups, piece = t.shape
    per_col = n_grp // n_atm
    if n_grp % n_atm or per_col % CORES:
        mine = lax.psum(t, "atm")
        full = lax.all_gather(mine, "grp", axis=0).transpose(2, 0, 1, 3).reshape(groups, -1)
        width = full.shape[1] // n_atm
        return mine, lax.dynamic_slice_in_dim(full, lax.axis_index("atm") * width, width, 1)
    half = per_col // CORES
    n_z = n_grp // CORES
    dma = pltpu.SemaphoreType.DMA
    vm = lambda *lead: pltpu.VMEM(lead + (groups, piece), jnp.float32)
    rows, cols = pl.pallas_call(
        functools.partial(gains_kernel, n_grp, n_atm, half),
        out_shape=(
            jax.ShapeDtypeStruct((n_atm, groups, piece), jnp.float32),
            jax.ShapeDtypeStruct((CORES, n_atm, half, groups, piece), jnp.float32),
        ),
        in_specs=[VM], out_specs=(VM, VM),
        scratch_shapes=[vm(n_atm - 1), vm(n_z)]
        + [dma((n_atm - 1,))] * 4 + [dma((n_z - 1,))] * 2 + [dma((n_atm - 1,))] * 2 + [dma((n_atm,))] * 2,
        compiler_params=pltpu.CompilerParams(collective_id=1, has_side_effects=True),
        name="share_gains",
    )(t)
    return rows, cols.transpose(3, 2, 0, 1, 4).reshape(groups, -1)


def gather_kernel(n_atm, v_ref, out_ref, s, r):
    col = lax.axis_index("atm")
    plane = [lax.rem(col + d, n_atm) for d in range(1, n_atm)]
    greet([{"atm": p} for p in plane])
    copies = [push(v_ref, out_ref.at[col], s, r, i, {"atm": p}) for i, p in enumerate(plane)]
    out_ref[col] = v_ref[...]
    for copy in copies:
        copy.wait()


def gather_atm(v, n_atm, ident):
    return pl.pallas_call(
        functools.partial(gather_kernel, n_atm),
        out_shape=jax.ShapeDtypeStruct((n_atm,) + v.shape, jnp.float32),
        in_specs=[VM], out_specs=VM,
        scratch_shapes=[pltpu.SemaphoreType.DMA((n_atm - 1,))] * 2,
        compiler_params=pltpu.CompilerParams(collective_id=ident, has_side_effects=True),
        name="gather_atm%d" % ident,
    )(v)


def split(value):
    high = value.astype(jnp.bfloat16)
    return high, (value - high.astype(jnp.float32)).astype(jnp.bfloat16)


def terms_kernel(groups, jac_ref, p_ref, out_ref, both):
    @pl.when(pl.program_id(0) == 0)
    def _():
        jac = jac_ref[...]
        high = jac.astype(jnp.bfloat16).astype(jnp.float32)
        both[...] = jnp.concatenate([high, jac - high], axis=0).T.astype(jnp.bfloat16)

    high, low = split(p_ref[...])
    one = jnp.dot(high, both[...], preferred_element_type=jnp.float32)
    two = jnp.dot(low, both[...], preferred_element_type=jnp.float32)
    one = one.T
    out_ref[0] = one[:groups] + one[groups:] + two.T[:groups]


def row_terms(covar, jac, n_atm):
    rows, width = covar.shape
    groups = jac.shape[0]
    piece = rows // n_atm
    tile = min(piece, 256)
    per = piece // tile
    return pl.pallas_call(
        functools.partial(terms_kernel, groups),
        grid=(rows // tile,),
        out_shape=jax.ShapeDtypeStruct((n_atm, groups, piece), jnp.float32),
        in_specs=[
            pl.BlockSpec((groups, width), lambda i: (0, 0)),
            pl.BlockSpec((tile, width), lambda i: (i, 0)),
        ],
        out_specs=pl.BlockSpec((1, groups, tile), lambda i: (i // per, 0, lax.rem(i, per))),
        scratch_shapes=[pltpu.VMEM((width, 2 * groups), jnp.bfloat16)],
        compiler_params=pltpu.CompilerParams(vmem_limit_bytes=48 << 20),
        name="row_terms",
    )(jac, covar)


def update_kernel(scale, left_ref, right_ref, p_ref, out_ref, right):
    @pl.when(pl.program_id(0) == 0)
    def _():
        high, low = split(right_ref[...])
        right[...] = jnp.concatenate([high, high, low], axis=0)

    high, low = split(left_ref[...])
    left = jnp.concatenate([high, low, high], axis=1)
    width = p_ref.shape[1]
    part = min(width, 512)
    for k in range(0, width, part):
        down = jnp.dot(left, right[:, k:k + part], preferred_element_type=jnp.float32)
        out_ref[:, k:k + part] = p_ref[:, k:k + part] * scale - down


def final_update(covar, left, right):
    rows, width = covar.shape
    depth = left.shape[1]
    tile = min(rows, 256)
    return pl.pallas_call(
        functools.partial(update_kernel, 1.0 / forget_rate ** STEPS),
        grid=(rows // tile,),
        out_shape=jax.ShapeDtypeStruct((rows, width), jnp.float32),
        in_specs=[
            pl.BlockSpec((tile, depth), lambda i: (i, 0)),
            pl.BlockSpec((depth, width), lambda i: (0, 0)),
            pl.BlockSpec((tile, width), lambda i: (i, 0)),
        ],
        out_specs=pl.BlockSpec((tile, width), lambda i: (i, 0)),
        scratch_shapes=[pltpu.VMEM((3 * depth, width), jnp.bfloat16)],
        compiler_params=pltpu.CompilerParams(vmem_limit_bytes=48 << 20),
        name="final_update",
    )(left, right, covar)


def body(atoms, kinds, member, targets, weights, bias, readout, covariance):
    n_grp, n_atm = lax.axis_size("grp"), lax.axis_size("atm")
    width = covariance.shape[1]
    groups = GROUP_LOCAL * n_grp
    identity = jnp.eye(groups, dtype=jnp.float32)
    dot = functools.partial(jnp.dot, precision=precise)
    current = weights
    past = []
    for step in range(STEPS):
        energies, partial_value = local_terms(
            atoms[step], kinds[step], member[step], current, bias, readout
        )
        blocks = partial_value.reshape(GROUP_LOCAL, n_atm, width).transpose(1, 0, 2)
        tail = jnp.broadcast_to(energies[None, :, None], (n_atm, GROUP_LOCAL, LANES))
        shared = share_grads(jnp.concatenate([blocks, tail], axis=2), n_grp, n_atm)
        shared = shared.reshape(groups, width + LANES)
        jac = shared[:, :width]
        mismatch = targets[step] - shared[:, width]
        terms = row_terms(covariance, jac, n_atm) * (1.0 / forget_rate ** step)
        for age, (rows_old, cols_old, inverse_old) in enumerate(past):
            small = lax.dot_general(jac, cols_old, (((1,), (1,)), ((), ())), precision=precise)
            small = dot(small, inverse_old) * (1.0 / forget_rate ** (step - age))
            terms = terms - jnp.einsum("xy,nyp->nxp", small, rows_old, precision=precise)
        rows, cols = share_gains(terms, n_grp, n_atm)
        part = lax.dot_general(jac, cols, (((1,), (1,)), ((), ())), precision=precise)
        curvature = jnp.sum(gather_atm(part, n_atm, 2), axis=0)
        innovation = 0.5 * (curvature + curvature.T) + forget_rate * identity
        factor = jnp.linalg.cholesky(innovation)
        inverse = jax.scipy.linalg.cho_solve((factor, True), identity)
        coefficient = dot(inverse, mismatch)
        change = dot(coefficient, cols).reshape(-1, current.shape[1])
        current = current + gather_atm(change, n_atm, 3).reshape(current.shape)
        past.append((rows, cols, inverse))
    left, right = [], []
    for age, (rows, cols, inverse) in enumerate(past):
        scaled = jnp.einsum("nxp,xy->npy", rows, inverse, precision=precise)
        left.append(scaled.reshape(-1, groups) * (1.0 / forget_rate ** (STEPS - age)))
        right.append(cols)
    covar = final_update(covariance, jnp.concatenate(left, axis=1), jnp.concatenate(right, axis=0))
    return (covar, current)


def solution(mesh):
    return jax.shard_map(
        body,
        mesh=mesh,
        in_specs=(
            P(None, ("grp", "atm"), None),
            P(None, ("grp", "atm")),
            P(None, ("grp", "atm")),
            P(),
            P(),
            P(),
            P(),
            P("grp", "atm"),
        ),
        out_specs=(P("grp", "atm"), P()),
        check_vma=False,
    )
```

time: 516 us -> 273 us (0.53); the launches traced: 508 us -> 271 us
  Pallas kernels: 0 us -> 200 us
  waiting for transfers between devices: 176 us -> 0 us
  matrix products: 170 us -> 17.2 us
  blocking collectives: 117 us -> 0 us
  local copies, waits for them, and re-layouts: 5.62 us -> 20.2 us
  between operations: 14.9 us -> 1.11 us
  other arithmetic: 24.9 us -> 33 us
    pallas_call x0 -> x11, Pallas kernels: none -> 200 us  [the longest x2 65.1 us: share_gains(): pl.pallas_call(functools.partial(gains_kernel, n_grp, n_atm, half), out_s...]
    dot_general x12 -> x11, matrix products: 165 us -> 11.9 us  [the longest x2 3.2 us: body(): lax.dot_general(jac, cols, (((1,), (1,)), ((), ())), precision=precise)]
    psum x4 -> x0, blocking collectives: 117 us -> none  [the longest x2 83.9 us: body(): predicted = lax.psum(spread, ('grp', 'atm'))]
    psum x2 -> x0, waiting for transfers between devices: 90.5 us -> none  [body(): row_gains = lax.psum(row_terms, 'atm')]
    reduce_scatter x2 -> x0, waiting for transfers between devices: 47.3 us -> none  [body(): lax.psum_scatter(partial_value, 'atm', scatter_dimension=1, tiled=True)]
    all_gather x4 -> x0, waiting for transfers between devices: 37.8 us -> none  [the longest x2 23.8 us: body(): grad_columns = lax.all_gather(grad_block, 'grp', axis=0, tiled=True)]
  transfers between devices with their start and end apart: 8 -> 0, of which waited for: 7 -> 0; matrix products, arithmetic and copies ran while one was open for 8% -> 0% of each run, Pallas kernels for 0% -> 0%
where the time goes in v1:
time: 273 us; the launch traced here: 271 us
  Pallas kernels  200 us (73%)
  other arithmetic  33 us (12%)
  local copies, waits for them, and re-layouts  20.2 us (7%)
  matrix products  17.2 us (6%)
    pallas_call x2, Pallas kernels, share_gains(): pl.pallas_call(functools.partial(gains_kernel, n_grp, n_atm, half), out_s...  65.1 us
    pallas_call x2, Pallas kernels, share_grads(): pl.pallas_call(functools.partial(grads_kernel, n_grp, n_atm), out_shape=j...  50 us
    pallas_call x2, Pallas kernels, row_terms(): pl.pallas_call(functools.partial(terms_kernel, groups), grid=(rows // til...  33.1 us
    pallas_call x1, Pallas kernels, final_update(): pl.pallas_call(functools.partial(update_kernel, 1.0 / forget_rate ** STEP...  26.2 us
    pallas_call x4, Pallas kernels, gather_atm(): pl.pallas_call(functools.partial(gather_kernel, n_atm), out_shape=jax.Sha...  25.1 us
    another operation x6, other arithmetic, body(): factor = jnp.linalg.cholesky(innovation)  13 us
    another operation x4, other arithmetic, body(): inverse = jax.scipy.linalg.cho_solve((factor, True), identity)  11.1 us

profile of v1, /device:TPU:0, one launch (start us, length us, event | category | flops | bytes accessed | tf_op | source)
XLA Modules:
  0.0 271.1 jit_solution(12930325041910441026)
XLA Ops:
  2.8 1.3 multiply_reduce_fusion.1
  7.8 26.8 %share_grads.2 = f32[8,8,4224]{2,1,0:T(8,128)} custom-call(f32[4,8,4224]{2,1,0:T(8,128)} %pad_maximum_fusion.2.x_ref), custom_call_target="tpu_custom_call" | custom-call | tf_op jit(solution)/shard_map/share_grads/pallas_call | solution.py:86
  34.6 1.4 slice_reduce_fusion.1
  36.0 1.3 slice.60.jac_ref
  37.3 16.5 %row_terms.2.t_ref = f32[4,64,512]{2,1,0:T(8,128)S(1)} custom-call(f32[64,4096]{1,0:T(8,128)S(1)} %slice.60.jac_ref, f32[2048,4096]{1,0:T(8,128)} %p_ref.5), custom_call_target="tpu_custom_call" | custom-call | tf_op jit(solution)/shard_map/row_terms/pallas_call | solution.py:201
  54.6 32.0 %share_gains.2 = (f32[4,64,512]{2,1,0:T(8,128)}, f32[2,4,1,64,512]{4,3,2,1,0:T(8,128)}) custom-call(f32[4,64,512]{2,1,0:T(8,128)} %copy-done.2), custom_call_target="tpu_custom_call" | custom-call | tf_op jit(solution)/shard_map/share_gains/pallas_call | solution.py:140
  86.7 1.9 copy.27
  89.8 1.6 fusion.61.v_ref
  91.4 6.5 %gather_atm2.2 = f32[4,64,64]{2,1,0:T(8,128)} custom-call(f32[64,64]{1,0:T(8,128)} %fusion.61.v_ref), custom_call_target="tpu_custom_call" | custom-call | tf_op jit(solution)/shard_map/gather_atm2/pallas_call | solution.py:166
  99.2 5.8 %cholesky.44 = f32[64,64]{1,0:T(8,128)S(1)} custom-call(f32[64,64]{1,0:T(8,128)S(1)} %fusion.49), custom_call_target="Cholesky" | custom-call | tf_op jit(solution)/shard_map/jit(cholesky)/cholesky | solution.py:278
  106.4 4.9 %custom-call.8 = f32[1,64,64]{1,2,0:T(8,128)S(1)} custom-call(f32[1,64,64]{2,1,0:T(8,128)S(1)} %fusion.37), custom_call_target="InvertDiagBlocksLowerTriangular" | custom-call | tf_op jit(solution)/shard_map/jit(_cho_solve)/triangular_solve | solution.py:279
  111.8 1.2 fusion.8
  113.1 6.0 %gather_atm3.2 = f32[4,32,128]{2,1,0:T(8,128)} custom-call(f32[32,128]{1,0:T(8,128)} %bitcast.173), custom_call_target="tpu_custom_call" | custom-call | tf_op jit(solution)/shard_map/gather_atm3/pallas_call | solution.py:166
  123.5 1.4 copy.31
  124.9 23.2 %share_grads.3 = f32[8,8,4224]{2,1,0:T(8,128)} custom-call(f32[4,8,4224]{2,1,0:T(8,128)} %pad_maximum_fusion.3.x_ref), custom_call_target="tpu_custom_call" | custom-call | tf_op jit(solution)/shard_map/share_grads/pallas_call | solution.py:86
  149.0 2.3 fusion.65
  151.6 16.6 %row_terms.3 = f32[4,64,512]{2,1,0:T(8,128)S(1)} custom-call(f32[64,4096]{1,0:T(8,128)S(1)} %slice.62.jac_ref, f32[2048,4096]{1,0:T(8,128)} %p_ref.5), custom_call_target="tpu_custom_call" | custom-call | tf_op jit(solution)/shard_map/row_terms/pallas_call | solution.py:201
  168.1 1.4 fusion.t_ref
  169.6 33.0 %share_gains.3 = (f32[4,64,512]{2,1,0:T(8,128)}, f32[2,4,1,64,512]{4,3,2,1,0:T(8,128)}) custom-call(f32[4,64,512]{2,1,0:T(8,128)} %fusion.t_ref), custom_call_target="tpu_custom_call" | custom-call | tf_op jit(solution)/shard_map/share_gains/pallas_call | solution.py:140
  202.6 2.9 %copy.35 = f32[64,1,2,4,512]{4,3,2,0,1:T(4,128)} copy(f32[64,1,2,4,512]{4,0,1,3,2:T(8,128)} %bitcast.171) | data formatting | bytes 2097152 | tf_op jit(solution)/shard_map/transpose | solution.py:152
  205.5 1.9 reshape.103
  207.4 1.6 fusion.63.v_ref
  209.0 6.4 %gather_atm2.3 = f32[4,64,64]{2,1,0:T(8,128)} custom-call(f32[64,64]{1,0:T(8,128)} %fusion.63.v_ref), custom_call_target="tpu_custom_call" | custom-call | tf_op jit(solution)/shard_map/gather_atm2/pallas_call | solution.py:166
  216.6 5.8 %cholesky.55 = f32[64,64]{1,0:T(8,128)S(1)} custom-call(f32[64,64]{1,0:T(8,128)S(1)} %fusion.43), custom_call_target="Cholesky" | custom-call | tf_op jit(solution)/shard_map/jit(cholesky)/cholesky | solution.py:278
  223.8 4.9 %custom-call.9 = f32[1,64,64]{1,2,0:T(8,128)S(1)} custom-call(f32[1,64,64]{2,1,0:T(8,128)S(1)} %fusion.38), custom_call_target="InvertDiagBlocksLowerTriangular" | custom-call | tf_op jit(solution)/shard_map/jit(_cho_solve)/triangular_solve | solution.py:279
  229.3 1.5 convolution_multiply_fusion
  232.0 1.4 pad_maximum_fusion.right_ref
  233.3 6.1 %gather_atm3.3 = f32[4,32,128]{2,1,0:T(8,128)} custom-call(f32[32,128]{1,0:T(8,128)} %bitcast.172), custom_call_target="tpu_custom_call" | custom-call | tf_op jit(solution)/shard_map/gather_atm3/pallas_call | solution.py:166
  239.5 1.5 bitcast_add_fusion
  241.0 2.4 copy.39
  243.3 1.6 pad_maximum_fusion.1.left_ref
  244.9 26.2 %final_update.1 = f32[2048,4096]{1,0:T(8,128)} custom-call(f32[2048,128]{1,0:T(8,128)S(1)} %pad_maximum_fusion.1.left_ref, f32[128,4096]{1,0:T(8,128)S(1)} %pad_maximum_fusion.right_ref, f32[2048,4096]{1,0:T(8,128)} %p_ref.5), custom_call_target="tpu_custom_call" | custom-call | tf_op jit(solution)/shard_map/final_update/pallas_call | solution.py:235
  (79 shorter events, 20.6 us)
Async XLA Ops:
  0.6 1.6 copy-start
  53.8 0.8 copy-start.2
  88.6 1.2 copy-start.5
  89.8 21.8 %copy-start.11 = (f32[2,64]{1,0:T(2,128)S(1)}, f32[2,64]{1,0:T(2,128)}, u32[]{:S(2)}) copy-start(f32[2,64]{1,0:T(2,128)} %param.14) | copy-start | bytes 1540
  89.8 21.9 %copy-start.12 = (f32[64]{0:T(128)S(1)}, f32[64]{0:T(128)}, u32[]{:S(2)}) copy-start(f32[64]{0:T(128)} %slice_reduce_fusion.1) | copy-start | bytes 772
  91.4 27.7 %copy-start.10 = (f32[128,128]{1,0:T(8,128)S(1)}, f32[128,128]{1,0:T(8,128)}, u32[]{:S(2)}) copy-start(f32[128,128]{1,0:T(8,128)} %param.15) | copy-start | bytes 196612
  98.0 22.0 %copy-start.8 = (f32[2,256,128]{2,1,0:T(8,128)S(1)}, f32[2,256,128]{2,1,0:T(8,128)}, u32[]{:S(2)}) copy-start(f32[2,256,128]{2,1,0:T(8,128)} %param.11) | copy-start | bytes 786436
  98.0 22.0 %copy-start.13 = (f32[128]{0:T(128)S(1)}, f32[128]{0:T(128)}, u32[]{:S(2)}) copy-start(f32[128]{0:T(128)} %param.16) | copy-start | bytes 1540
  121.7 1.2 copy-start.7
  149.0 2.5 copy-start.3
  207.4 23.3 %copy-start.4 = (f32[64,4096]{1,0:T(8,128)}, f32[64,4096]{1,0:T(8,128)S(1)}, u32[]{:S(2)}) copy-start(f32[64,4096]{1,0:T(8,128)S(1)} %reshape.103) | copy-start | bytes 3145732
  209.0 20.2 %copy-start.9 = (f32[4,64,512]{2,1,0:T(8,128)S(1)}, f32[4,64,512]{2,1,0:T(8,128)}, u32[]{:S(2)}) copy-start(f32[4,64,512]{2,1,0:T(8,128)} %get-tuple-element.10) | copy-start | bytes 1572868
  233.3 10.0 %copy-start.6 = (f32[4,512,64]{2,1,0:T(8,128)S(1)}, f32[4,512,64]{2,1,0:T(8,128)}, u32[]{:S(2)}) copy-start(f32[4,512,64]{2,1,0:T(8,128)} %copy.31) | copy-start | bytes 1572868
  244.9 26.3 %copy-start.1 = (f32[4,128]{1,0:T(4,128)S(1)}, f32[4,128]{1,0:T(4,128)}, u32[]{:S(2)}) copy-start(f32[4,128]{1,0:T(4,128)} %param.17) | copy-start | bytes 6148

commit v2 on v1

--- a/solution.py
+++ b/solution.py
@@ -10,6 +10,7 @@
 STEPS = 2
 CORES = 2
 LANES = 128
+CHUNKS = 2
 
 forget_rate = 0.98
 precise = lax.Precision.HIGHEST
@@ -60,22 +61,31 @@
 def grads_kernel(n_grp, n_atm, x_ref, out_ref, got, a_s, a_r, b_s, b_r, f_s, f_r):
     row, col, z, core, plane, column, partner = places(n_grp, n_atm)
     greet([{"atm": p} for p in plane] + [{"grp": p} for p in column] + [{"grp": partner}])
-    first = [push(x_ref.at[p], got.at[i], a_s, a_r, i, {"atm": p}) for i, p in enumerate(plane)]
-    total = x_ref[col]
-    for i, copy in enumerate(first):
-        copy.wait_recv()
-        total = total + got[i]
-    out_ref[row] = total
-    second = [push(out_ref.at[row], out_ref.at[row], b_s, b_r, i, {"grp": p}) for i, p in enumerate(column)]
-    last = [push(out_ref.at[row], out_ref.at[row], f_s, f_r, len(column), {"grp": partner})]
     n_z = n_grp // CORES
-    for i, copy in enumerate(second):
-        copy.wait_recv()
-        origin = lax.rem(z + n_z - (i + 1), n_z) * CORES + core
-        last.append(push(out_ref.at[origin], out_ref.at[origin], f_s, f_r, i, {"grp": partner}))
+    wide = x_ref.shape[2]
+    middle = wide // 2 // LANES * LANES
+    cuts = [pl.ds(0, middle), pl.ds(middle, wide - middle)]
+    first, second, last = [], [], []
+    for k, cut in enumerate(cuts):
+        first.append([push(x_ref.at[p, :, cut], got.at[i, :, cut], a_s.at[k], a_r.at[k], i, {"atm": p}) for i, p in enumerate(plane)])
+    for k, cut in enumerate(cuts):
+        total = x_ref[col, :, cut]
+        for i, copy in enumerate(first[k]):
+            copy.wait_recv()
+            total = total + got[i, :, cut]
+        out_ref[row, :, cut] = total
+        place = out_ref.at[row, :, cut]
+        second.append([push(place, place, b_s.at[k], b_r.at[k], i, {"grp": p}) for i, p in enumerate(column)])
+        last.append(push(place, place, f_s.at[k], f_r.at[k], len(column), {"grp": partner}))
+    for k, cut in enumerate(cuts):
+        for i, copy in enumerate(second[k]):
+            copy.wait_recv()
+            origin = lax.rem(z + n_z - (i + 1), n_z) * CORES + core
+            place = out_ref.at[origin, :, cut]
+            last.append(push(place, place, f_s.at[k], f_r.at[k], i, {"grp": partner}))
     for copy in last:
         copy.wait_recv()
-    for copy in first + second + last:
+    for copy in sum(first + second, last):
         copy.wait_send()
 
 
@@ -88,7 +98,7 @@
         out_shape=jax.ShapeDtypeStruct((n_grp,) + block, jnp.float32),
         in_specs=[VM], out_specs=VM,
         scratch_shapes=[pltpu.VMEM((n_atm - 1,) + block, jnp.float32)]
-        + [dma((n_atm - 1,))] * 2 + [dma((n_z - 1,))] * 2 + [dma((n_z,))] * 2,
+        + [dma((2, n_atm - 1))] * 2 + [dma((2, n_z - 1))] * 2 + [dma((2, n_z))] * 2,
         compiler_params=pltpu.CompilerParams(collective_id=0, has_side_effects=True),
         name="share_grads",
     )(x)
@@ -98,31 +108,43 @@
                  a_s, a_r, r_s, r_r, b_s, b_r, c_s, c_r, f_s, f_r):
     row, col, z, core, plane, column, partner = places(n_grp, n_atm)
     greet([{"atm": p} for p in plane] + [{"grp": p} for p in column] + [{"grp": partner}])
-    first = [push(t_ref.at[p], got.at[i], a_s, a_r, i, {"atm": p}) for i, p in enumerate(plane)]
-    total = t_ref[col]
-    for i, copy in enumerate(first):
-        copy.wait_recv()
-        total = total + got[i]
-    quarter[z] = total
-    row_ref[col] = total
-    along = [push(quarter.at[z], quarter.at[z], b_s, b_r, i, {"grp": p}) for i, p in enumerate(column)]
-    rows = [push(row_ref.at[col], row_ref.at[col], r_s, r_r, i, {"atm": p}) for i, p in enumerate(plane)]
-    for copy in along:
-        copy.wait_recv()
-    across = [
-        push(quarter.at[pl.ds(p * half, half)], col_ref.at[core, col], c_s, c_r, i, {"atm": p})
-        for i, p in enumerate(plane)
-    ]
-    col_ref[core, col] = quarter[pl.ds(col * half, half)]
-    last = [push(col_ref.at[core, col], col_ref.at[core, col], f_s, f_r, len(plane), {"grp": partner})]
-    for i, copy in enumerate(across):
-        copy.wait_recv()
-        origin = lax.rem(col + n_atm - (i + 1), n_atm)
-        last.append(push(col_ref.at[core, origin], col_ref.at[core, origin], f_s, f_r, i, {"grp": partner}))
-    for copy in rows + last:
-        copy.wait_recv()
-    for copy in first + along + rows + across + last:
-        copy.wait_send()
+    groups = t_ref.shape[1]
+    chunk = groups // CHUNKS
+    cuts = [pl.ds(k * chunk, chunk) for k in range(CHUNKS)]
+    first, along, rows, across, last = [], [], [], [], []
+    for k, cut in enumerate(cuts):
+        first.append([push(t_ref.at[p, cut], got.at[i, cut], a_s.at[k], a_r.at[k], i, {"atm": p}) for i, p in enumerate(plane)])
+    for k, cut in enumerate(cuts):
+        total = t_ref[col, cut]
+        for i, copy in enumerate(first[k]):
+            copy.wait_recv()
+            total = total + got[i, cut]
+        quarter[z, cut] = total
+        row_ref[col, cut] = total
+        along.append([push(quarter.at[z, cut], quarter.at[z, cut], b_s.at[k], b_r.at[k], i, {"grp": p}) for i, p in enumerate(column)])
+        rows.append([push(row_ref.at[col, cut], row_ref.at[col, cut], r_s.at[k], r_r.at[k], i, {"atm": p}) for i, p in enumerate(plane)])
+    for k, cut in enumerate(cuts):
+        for copy in along[k]:
+            copy.wait_recv()
+        across.append([
+            push(quarter.at[pl.ds(p * half, half), cut], col_ref.at[core, col, :, cut], c_s.at[k], c_r.at[k], i, {"atm": p})
+            for i, p in enumerate(plane)
+        ])
+        col_ref[core, col, :, cut] = quarter[pl.ds(col * half, half), cut]
+        place = col_ref.at[core, col, :, cut]
+        last.append([push(place, place, f_s.at[k], f_r.at[k], len(plane), {"grp": partner})])
+    for k, cut in enumerate(cuts):
+        for i, copy in enumerate(across[k]):
+            copy.wait_recv()
+            origin = lax.rem(col + n_atm - (i + 1), n_atm)
+            place = col_ref.at[core, origin, :, cut]
+            last[k].append(push(place, place, f_s.at[k], f_r.at[k], i, {"grp": partner}))
+    for group in rows + last:
+        for copy in group:
+            copy.wait_recv()
+    for group in first + along + rows + across + last:
+        for copy in group:
+            copy.wait_send()
 
 
 def share_gains(t, n_grp, n_atm):
@@ -145,7 +167,7 @@
         ),
         in_specs=[VM], out_specs=(VM, VM),
         scratch_shapes=[vm(n_atm - 1), vm(n_z)]
-        + [dma((n_atm - 1,))] * 4 + [dma((n_z - 1,))] * 2 + [dma((n_atm - 1,))] * 2 + [dma((n_atm,))] * 2,
+        + [dma((CHUNKS, n_atm - 1))] * 4 + [dma((CHUNKS, n_z - 1))] * 2 + [dma((CHUNKS, n_atm - 1))] * 2 + [dma((CHUNKS, n_atm))] * 2,
         compiler_params=pltpu.CompilerParams(collective_id=1, has_side_effects=True),
         name="share_gains",
     )(t)
@@ -171,6 +193,42 @@
         compiler_params=pltpu.CompilerParams(collective_id=ident, has_side_effects=True),
         name="gather_atm%d" % ident,
     )(v)
+
+
+def inverse_kernel(parts_ref, out_ref, work):
+    size = out_ref.shape[0]
+    total = parts_ref[0]
+    for k in range(1, parts_ref.shape[0]):
+        total = total + parts_ref[k]
+    down = lax.broadcasted_iota(jnp.int32, (size, size), 0)
+    over = lax.broadcasted_iota(jnp.int32, (size, size), 1)
+    work[...] = 0.5 * (total + total.T) + jnp.where(down == over, forget_rate, 0.0)
+
+    def sweep(k, carry):
+        full = work[...]
+        row = work[pl.ds(k, 1), :]
+        column = jnp.sum(jnp.where(over == k, full, 0.0), axis=1, keepdims=True)
+        pivot = 1.0 / jnp.sum(jnp.where(over[:1] == k, row, 0.0), axis=1, keepdims=True)
+        row_part, col_part = row * pivot, column * pivot
+        swept = full - column * row_part
+        swept = jnp.where(down == k, row_part, swept)
+        swept = jnp.where(over == k, col_part, swept)
+        work[...] = jnp.where((down == k) & (over == k), -pivot, swept)
+        return carry
+
+    lax.fori_loop(0, size, sweep, 0)
+    out_ref[...] = -work[...]
+
+
+def innovation_inverse(parts):
+    size = parts.shape[-1]
+    return pl.pallas_call(
+        inverse_kernel,
+        out_shape=jax.ShapeDtypeStruct((size, size), jnp.float32),
+        in_specs=[VM], out_specs=VM,
+        scratch_shapes=[pltpu.VMEM((size, size), jnp.float32)],
+        name="innovation_inverse",
+    )(parts)
 
 
 def split(value):
@@ -252,7 +310,6 @@
     n_grp, n_atm = lax.axis_size("grp"), lax.axis_size("atm")
     width = covariance.shape[1]
     groups = GROUP_LOCAL * n_grp
-    identity = jnp.eye(groups, dtype=jnp.float32)
     dot = functools.partial(jnp.dot, precision=precise)
     current = weights
     past = []
@@ -273,10 +330,7 @@
             terms = terms - jnp.einsum("xy,nyp->nxp", small, rows_old, precision=precise)
         rows, cols = share_gains(terms, n_grp, n_atm)
         part = lax.dot_general(jac, cols, (((1,), (1,)), ((), ())), precision=precise)
-        curvature = jnp.sum(gather_atm(part, n_atm, 2), axis=0)
-        innovation = 0.5 * (curvature + curvature.T) + forget_rate * identity
-        factor = jnp.linalg.cholesky(innovation)
-        inverse = jax.scipy.linalg.cho_solve((factor, True), identity)
+        inverse = innovation_inverse(gather_atm(part, n_atm, 2))
         coefficient = dot(inverse, mismatch)
         change = dot(coefficient, cols).reshape(-1, current.shape[1])
         current = current + gather_atm(change, n_atm, 3).reshape(current.shape)

time: 273 us -> 251 us (0.919)
  other arithmetic: 33 us -> 7.07 us
  Pallas kernels: 200 us -> 203 us
    another operation x10 -> x0, other arithmetic: 24.1 us -> none  [the longest x6 13 us: body(): factor = jnp.linalg.cholesky(innovation)]
    pallas_call x0 -> x2, Pallas kernels: none -> 15.8 us  [innovation_inverse(): pl.pallas_call(inverse_kernel, out_shape=jax.ShapeDtypeStruct((size, size...]
    pallas_call x2, Pallas kernels: 65.1 us -> 55.7 us  [share_gains(): pl.pallas_call(functools.partial(gains_kernel, n_grp, n_atm, half), out_s...]
    pallas_call x2, Pallas kernels: 50 us -> 46.8 us  [share_grads(): pl.pallas_call(functools.partial(grads_kernel, n_grp, n_atm), out_shape=j...]
where the time goes in v2:
time: 251 us; the launch traced here: 250 us
  Pallas kernels  203 us (81%)
  local copies, waits for them, and re-layouts  19.4 us (8%)
  matrix products  19 us (8%)
  other arithmetic  7.07 us (3%)
    pallas_call x2, Pallas kernels, share_gains(): pl.pallas_call(functools.partial(gains_kernel, n_grp, n_atm, half), out_s...  55.7 us
    pallas_call x2, Pallas kernels, share_grads(): pl.pallas_call(functools.partial(grads_kernel, n_grp, n_atm), out_shape=j...  46.8 us
    pallas_call x2, Pallas kernels, row_terms(): pl.pallas_call(functools.partial(terms_kernel, groups), grid=(rows // til...  33.1 us
    pallas_call x1, Pallas kernels, final_update(): pl.pallas_call(functools.partial(update_kernel, 1.0 / forget_rate ** STEP...  26.3 us
    pallas_call x4, Pallas kernels, gather_atm(): pl.pallas_call(functools.partial(gather_kernel, n_atm), out_shape=jax.Sha...  25.5 us
    pallas_call x2, Pallas kernels, innovation_inverse(): pl.pallas_call(inverse_kernel, out_shape=jax.ShapeDtypeStruct((size, size...  15.8 us

profile of v2, /device:TPU:0, one launch (start us, length us, event | category | flops | bytes accessed | tf_op | source)
XLA Modules:
  0.0 249.6 jit_solution(12829471932681791359)
XLA Ops:
  2.8 1.3 multiply_reduce_fusion.1
  4.3 1.0 slice_bitcast_fusion
  7.8 24.6 %share_grads.2 = f32[8,8,4224]{2,1,0:T(8,128)} custom-call(f32[4,8,4224]{2,1,0:T(8,128)} %pad_maximum_fusion.2.x_ref), custom_call_target="tpu_custom_call" | custom-call | tf_op jit(solution)/shard_map/share_grads/pallas_call | solution.py:96
  33.3 1.3 slice.48.jac_ref
  34.7 16.5 %row_terms.2.t_ref = f32[4,64,512]{2,1,0:T(8,128)S(1)} custom-call(f32[64,4096]{1,0:T(8,128)S(1)} %slice.48.jac_ref, f32[2048,4096]{1,0:T(8,128)} %p_ref.5), custom_call_target="tpu_custom_call" | custom-call | tf_op jit(solution)/shard_map/row_terms/pallas_call | solution.py:259
  52.0 28.3 %share_gains.2 = (f32[4,64,512]{2,1,0:T(8,128)}, f32[2,4,1,64,512]{4,3,2,1,0:T(8,128)}) custom-call(f32[4,64,512]{2,1,0:T(8,128)} %copy-done.2), custom_call_target="tpu_custom_call" | custom-call | tf_op jit(solution)/shard_map/share_gains/pallas_call | solution.py:162
  80.3 1.9 copy.23
  83.4 1.6 fusion.45.v_ref
  85.0 6.5 %gather_atm2.2.parts_ref = f32[4,64,64]{2,1,0:T(8,128)} custom-call(f32[64,64]{1,0:T(8,128)} %fusion.45.v_ref), custom_call_target="tpu_custom_call" | custom-call | tf_op jit(solution)/shard_map/gather_atm2/pallas_call | solution.py:188
  91.5 7.9 %innovation_inverse.2 = f32[64,64]{1,0:T(8,128)} custom-call(f32[4,64,64]{2,1,0:T(8,128)} %gather_atm2.2.parts_ref), custom_call_target="tpu_custom_call" | custom-call | tf_op jit(solution)/shard_map/innovation_inverse/pallas_call | solution.py:225
  100.3 1.2 fusion.8
  101.6 6.0 %gather_atm3.2 = f32[4,32,128]{2,1,0:T(8,128)} custom-call(f32[32,128]{1,0:T(8,128)} %bitcast.137), custom_call_target="tpu_custom_call" | custom-call | tf_op jit(solution)/shard_map/gather_atm3/pallas_call | solution.py:188
  109.0 1.0 fusion.11
  112.0 1.4 copy.25
  113.4 22.2 %share_grads.3 = f32[8,8,4224]{2,1,0:T(8,128)} custom-call(f32[4,8,4224]{2,1,0:T(8,128)} %pad_maximum_fusion.3.x_ref), custom_call_target="tpu_custom_call" | custom-call | tf_op jit(solution)/shard_map/share_grads/pallas_call | solution.py:96
  136.5 2.3 fusion.49
  139.0 16.6 %row_terms.3 = f32[4,64,512]{2,1,0:T(8,128)S(1)} custom-call(f32[64,4096]{1,0:T(8,128)S(1)} %slice.50.jac_ref, f32[2048,4096]{1,0:T(8,128)} %p_ref.5), custom_call_target="tpu_custom_call" | custom-call | tf_op jit(solution)/shard_map/row_terms/pallas_call | solution.py:259
  155.6 1.5 fusion.t_ref
  157.0 27.4 %share_gains.3 = (f32[4,64,512]{2,1,0:T(8,128)}, f32[2,4,1,64,512]{4,3,2,1,0:T(8,128)}) custom-call(f32[4,64,512]{2,1,0:T(8,128)} %fusion.t_ref), custom_call_target="tpu_custom_call" | custom-call | tf_op jit(solution)/shard_map/share_gains/pallas_call | solution.py:162
  184.5 2.9 %copy.29 = f32[64,1,2,4,512]{4,3,2,0,1:T(4,128)} copy(f32[64,1,2,4,512]{4,0,1,3,2:T(8,128)} %bitcast.135) | data formatting | bytes 2097152 | tf_op jit(solution)/shard_map/transpose | solution.py:174
  187.4 1.9 reshape.93
  189.3 1.6 fusion.47.v_ref
  190.9 6.8 %gather_atm2.3.parts_ref = f32[4,64,64]{2,1,0:T(8,128)} custom-call(f32[64,64]{1,0:T(8,128)} %fusion.47.v_ref), custom_call_target="tpu_custom_call" | custom-call | tf_op jit(solution)/shard_map/gather_atm2/pallas_call | solution.py:188
  197.7 7.9 %innovation_inverse.3 = f32[64,64]{1,0:T(8,128)} custom-call(f32[4,64,64]{2,1,0:T(8,128)} %gather_atm2.3.parts_ref), custom_call_target="tpu_custom_call" | custom-call | tf_op jit(solution)/shard_map/innovation_inverse/pallas_call | solution.py:225
  206.5 2.5 %convolution_multiply_fusion = f32[4,512,64]{1,2,0:T(8,128)} fusion(f32[4,64,512]{2,1,0:T(8,128)} %get-tuple-element.8, f32[64,64]{1,0:T(8,128)} %innovation_inverse.3), kind=kOutput, calls=%fused_computation.3 | convolution fusion | flops 100794368 | bytes 1064960 | tf_op jit(solution)/shard_map/nxp,xy->npy/dot_general | solution.py:340
  209.0 1.2 fusion.5
  210.2 1.5 pad_maximum_fusion.right_ref
  211.7 6.2 %gather_atm3.3 = f32[4,32,128]{2,1,0:T(8,128)} custom-call(f32[32,128]{1,0:T(8,128)} %bitcast.136), custom_call_target="tpu_custom_call" | custom-call | tf_op jit(solution)/shard_map/gather_atm3/pallas_call | solution.py:188
  218.0 1.5 bitcast_add_fusion
  219.4 2.4 copy.31
  221.8 1.6 pad_maximum_fusion.1.left_ref
  223.4 26.3 %final_update.1 = f32[2048,4096]{1,0:T(8,128)} custom-call(f32[2048,128]{1,0:T(8,128)S(1)} %pad_maximum_fusion.1.left_ref, f32[128,4096]{1,0:T(8,128)S(1)} %pad_maximum_fusion.right_ref, f32[2048,4096]{1,0:T(8,128)} %p_ref.5), custom_call_target="tpu_custom_call" | custom-call | tf_op jit(solution)/shard_map/final_update/pallas_call | solution.py:293
  (55 shorter events, 14.0 us)
Async XLA Ops:
  0.6 1.6 copy-start
  51.2 0.8 copy-start.2
  82.2 1.2 copy-start.5
  83.4 16.0 %copy-start.11 = (f32[2,64]{1,0:T(2,128)S(1)}, f32[2,64]{1,0:T(2,128)}, u32[]{:S(2)}) copy-start(f32[2,64]{1,0:T(2,128)} %param.11) | copy-start | bytes 1540
  85.0 22.6 %copy-start.10 = (f32[128,128]{1,0:T(8,128)S(1)}, f32[128,128]{1,0:T(8,128)}, u32[]{:S(2)}) copy-start(f32[128,128]{1,0:T(8,128)} %param.12) | copy-start | bytes 196612
  85.0 23.5 %copy-start.8 = (f32[2,256,128]{2,1,0:T(8,128)S(1)}, f32[2,256,128]{2,1,0:T(8,128)}, u32[]{:S(2)}) copy-start(f32[2,256,128]{2,1,0:T(8,128)} %param.8) | copy-start | bytes 786436
  85.0 23.5 %copy-start.12 = (f32[128]{0:T(128)S(1)}, f32[128]{0:T(128)}, u32[]{:S(2)}) copy-start(f32[128]{0:T(128)} %param.13) | copy-start | bytes 1540
  110.2 1.2 copy-start.7
  110.2 1.2 copy-start.9
  136.5 2.5 copy-start.3
  189.3 19.7 %copy-start.4 = (f32[64,4096]{1,0:T(8,128)}, f32[64,4096]{1,0:T(8,128)S(1)}, u32[]{:S(2)}) copy-start(f32[64,4096]{1,0:T(8,128)S(1)} %reshape.93) | copy-start | bytes 3145732
  211.7 10.1 %copy-start.6 = (f32[4,512,64]{2,1,0:T(8,128)S(1)}, f32[4,512,64]{2,1,0:T(8,128)}, u32[]{:S(2)}) copy-start(f32[4,512,64]{2,1,0:T(8,128)} %copy.25) | copy-start | bytes 1572868
  223.4 26.3 %copy-start.1 = (f32[4,128]{1,0:T(4,128)S(1)}, f32[4,128]{1,0:T(4,128)}, u32[]{:S(2)}) copy-start(f32[4,128]{1,0:T(4,128)} %param.14) | copy-start | bytes 6148
